TPU v7x, 32 devices: a whole 2x2x4 slice. The times are simulated.
32 devices in a mesh: dp: 8 (over z, y), tensor: 4 (over x, core).
Axes of the slice: x: 2, y: 2, z: 4, core: 2. Of those that a mesh axis runs over, the one named last changes fastest.
Arguments:
- tokens: bfloat16 [4096, 2048], P(('dp', 'tensor')), may hold values from -6 to 6
- lengths: int32 [8, 4], P('dp'), may hold values from 0 to 512, as said below
- w_query: bfloat16 [2048, 2048], P(None, 'tensor'), may hold values from -0.125 to 0.125
- w_key: bfloat16 [2048, 2048], P(None, 'tensor'), may hold values from -0.125 to 0.125
- w_value: bfloat16 [2048, 2048], P(None, 'tensor'), may hold values from -0.125 to 0.125
- w_out: bfloat16 [2048, 2048], P('tensor'), may hold values from -0.125 to 0.125
- w_gate: bfloat16 [2048, 8192], P(None, 'tensor'), may hold values from -0.125 to 0.125
- w_up: bfloat16 [2048, 8192], P(None, 'tensor'), may hold values from -0.125 to 0.125
- w_down: bfloat16 [8192, 2048], P('tensor'), may hold values from -0.0625 to 0.0625
- gain_query: float32 [2048], P('tensor'), may hold values from 0.1 to 1.9
- gain_key: float32 [2048], P('tensor'), may hold values from 0.1 to 1.9
- gain_attn: float32 [2048], replicated, may hold values from 0.1 to 1.9
- gain_mlp: float32 [2048], replicated, may hold values from 0.1 to 1.9
- cotangent: bfloat16 [4096, 2048], P(('dp', 'tensor')), may hold values from -6 to 6
Outputs:
- output: bfloat16 [4096, 2048], P(('dp', 'tensor'))
- grad_tokens: bfloat16 [4096, 2048], P(('dp', 'tensor'))
- grad_w_query: float32 [2048, 2048], P('dp', 'tensor')
- grad_w_key: float32 [2048, 2048], P('dp', 'tensor')
- grad_w_value: float32 [2048, 2048], P('dp', 'tensor')
- grad_w_out: float32 [2048, 2048], P('tensor', 'dp')
- grad_w_gate: float32 [2048, 8192], P('dp', 'tensor')
- grad_w_up: float32 [2048, 8192], P('dp', 'tensor')
- grad_w_down: float32 [8192, 2048], P('tensor', 'dp')
- grad_gain_query: float32 [2048], P('tensor')
- grad_gain_key: float32 [2048], P('tensor')
- grad_gain_attn: float32 [2048], replicated
- grad_gain_mlp: float32 [2048], replicated
Inputs may be any that keep to these rules, and one draw needn't show every extreme that they name: Each row lists the lengths of its sequences in order, then zeros; every nonzero length is 128 or more and they sum to 512; row 0 holds one sequence of 512 tokens.
All inputs are finite; a program needn't handle non-finite values.
Results may differ from a plain program's by a relative error of at most 0.023.
Values may be sent and summed in bfloat16 or wider, within the bound.
A program may use at most 256 MiB of HBM per device.

v0:
```python
import math
import jax
import jax.numpy as jnp
from jax import lax
from jax.sharding import PartitionSpec as P

HD = 128
ROW_LEN = 512
EPS = 1e-06
THETA = 500000.0


def rotate(values, offsets, rot_sign):
    half_width = values.shape[-1] // 2
    frequency = jnp.exp(
        jnp.arange(half_width, dtype=jnp.float32) * (-2.0 * math.log(THETA) / values.shape[-1])
    )
    angles = offsets.astype(jnp.float32)[..., None, None] * frequency
    cosines = jnp.cos(angles)
    sine_part = rot_sign * jnp.sin(angles)
    first_half = values[..., :half_width]
    second_half = values[..., half_width:]
    return jnp.concatenate(
        [
            first_half * cosines - second_half * sine_part,
            second_half * cosines + first_half * sine_part,
        ],
        axis=-1,
    )


def row_layout(lengths_row):
    seq_ends = jnp.cumsum(lengths_row)
    position = jnp.arange(ROW_LEN, dtype=jnp.int32)
    passed = (position[:, None] >= seq_ends[None, :]).astype(jnp.int32)
    segment = jnp.sum(passed, axis=1)
    seq_start = jnp.sum(passed * lengths_row[None, :], axis=1)
    return (segment, position - seq_start)


def allowed_mask(segment):
    position = jnp.arange(segment.shape[0], dtype=jnp.int32)
    return (segment[:, None] == segment[None, :]) & (position[None, :] <= position[:, None])


def times_t(left_mat, right_mat):
    return lax.dot_general(
        left_mat, right_mat, (((1,), (1,)), ((), ())), preferred_element_type=jnp.float32
    )


def t_times(left_mat, right_mat):
    return lax.dot_general(
        left_mat, right_mat, (((0,), (0,)), ((), ())), preferred_element_type=jnp.float32
    )


def masked_scores(queries_low, keys_low, segment):
    scale_factor = 1.0 / math.sqrt(queries_low.shape[-1])
    scores = (
        jnp.einsum("qhd,khd->hqk", queries_low, keys_low, preferred_element_type=jnp.float32)
        * scale_factor
    )
    return jnp.where(allowed_mask(segment)[None], scores, -1e30)


def attend(block_item):
    queries_low, keys_low, values_low, segment = block_item
    scores = masked_scores(queries_low, keys_low, segment)
    row_max = jnp.max(scores, axis=-1, keepdims=True)
    shifted = jnp.exp(scores - row_max)
    row_total = jnp.sum(shifted, axis=-1, keepdims=True)
    attn_weights = (shifted / row_total).astype(jnp.bfloat16)
    mixed = jnp.einsum("hqk,khd->qhd", attn_weights, values_low, preferred_element_type=jnp.float32)
    return (mixed.astype(jnp.bfloat16), (row_max + jnp.log(row_total))[..., 0])


def attend_back(block_item):
    queries_low, keys_low, values_low, segment, log_total, grad_mixed = block_item
    scale_factor = 1.0 / math.sqrt(queries_low.shape[-1])
    scores = masked_scores(queries_low, keys_low, segment)
    attn_weights = jnp.exp(scores - log_total[..., None])
    grad_weights = jnp.einsum(
        "qhd,khd->hqk", grad_mixed, values_low, preferred_element_type=jnp.float32
    )
    row_dots = jnp.sum(attn_weights * grad_weights, axis=-1, keepdims=True)
    grad_scores = (attn_weights * (grad_weights - row_dots)).astype(jnp.bfloat16)
    grad_queries = scale_factor * jnp.einsum(
        "hqk,khd->qhd", grad_scores, keys_low, preferred_element_type=jnp.float32
    )
    grad_keys = scale_factor * jnp.einsum(
        "hqk,qhd->khd", grad_scores, queries_low, preferred_element_type=jnp.float32
    )
    grad_values = jnp.einsum(
        "hqk,qhd->khd",
        attn_weights.astype(jnp.bfloat16),
        grad_mixed,
        preferred_element_type=jnp.float32,
    )
    return (grad_queries, grad_keys, grad_values.astype(jnp.bfloat16))


def post_norm_back(grad_in, unit_rows, inv_scale, gain_vec):
    scaled = grad_in * gain_vec
    mean_dots = jnp.mean(scaled * unit_rows, axis=-1, keepdims=True)
    return (inv_scale * (scaled - unit_rows * mean_dots), jnp.sum(grad_in * unit_rows, axis=0))


def body(
    tokens,
    lengths,
    w_query,
    w_key,
    w_value,
    w_out,
    w_gate,
    w_up,
    w_down,
    gain_query,
    gain_key,
    gain_attn,
    gain_mlp,
    cotangent,
):
    rows_dev = lengths.shape[0]
    model_width = w_query.shape[0]
    local_width = w_query.shape[1]
    head_count = local_width // HD
    gathered = lax.all_gather(tokens, "tensor", axis=0, tiled=True)
    row_count = gathered.shape[0]
    segment, offsets = jax.vmap(row_layout)(lengths)
    queries = jnp.dot(gathered, w_query, preferred_element_type=jnp.float32)
    keys_raw = jnp.dot(gathered, w_key, preferred_element_type=jnp.float32)
    values_low = jnp.dot(gathered, w_value, preferred_element_type=jnp.float32).astype(jnp.bfloat16)
    q_total, k_total = lax.psum(
        (jnp.sum(queries * queries, axis=1), jnp.sum(keys_raw * keys_raw, axis=1)), "tensor"
    )
    q_inv = lax.rsqrt(q_total / model_width + EPS)[:, None]
    k_inv = lax.rsqrt(k_total / model_width + EPS)[:, None]
    q_unit = queries * q_inv
    k_unit = keys_raw * k_inv

    def to_heads(values):
        return values.reshape(rows_dev, ROW_LEN, head_count, HD)

    queries_low = rotate(to_heads(q_unit * gain_query), offsets, 1.0).astype(jnp.bfloat16)
    keys_low = rotate(to_heads(k_unit * gain_key), offsets, 1.0).astype(jnp.bfloat16)
    values_heads = to_heads(values_low)
    mixed_heads, log_total = lax.map(attend, (queries_low, keys_low, values_heads, segment))
    mixed_low = mixed_heads.reshape(row_count, local_width)
    attn_out = lax.psum_scatter(
        jnp.dot(mixed_low, w_out, preferred_element_type=jnp.float32).astype(jnp.bfloat16),
        "tensor",
        scatter_dimension=0,
        tiled=True,
    ).astype(jnp.float32)
    a_inv = lax.rsqrt(jnp.mean(attn_out * attn_out, axis=1, keepdims=True) + EPS)
    a_unit = attn_out * a_inv
    hidden = tokens.astype(jnp.float32) + a_unit * gain_attn
    hidden_all = lax.all_gather(hidden.astype(jnp.bfloat16), "tensor", axis=0, tiled=True)
    gate_acts = jnp.dot(hidden_all, w_gate, preferred_element_type=jnp.float32)
    up_acts = jnp.dot(hidden_all, w_up, preferred_element_type=jnp.float32)
    gate_sigmoid = jax.nn.sigmoid(gate_acts)
    inner_low = (gate_acts * gate_sigmoid * up_acts).astype(jnp.bfloat16)
    mlp_out = lax.psum_scatter(
        jnp.dot(inner_low, w_down, preferred_element_type=jnp.float32).astype(jnp.bfloat16),
        "tensor",
        scatter_dimension=0,
        tiled=True,
    ).astype(jnp.float32)
    f_inv = lax.rsqrt(jnp.mean(mlp_out * mlp_out, axis=1, keepdims=True) + EPS)
    f_unit = mlp_out * f_inv
    output = (hidden + f_unit * gain_mlp).astype(jnp.bfloat16)
    grad_output = cotangent.astype(jnp.float32)
    grad_mlp, grad_gain_mlp_part = post_norm_back(grad_output, f_unit, f_inv, gain_mlp)
    mlp_grad_all = lax.all_gather(grad_mlp.astype(jnp.bfloat16), "tensor", axis=0, tiled=True)
    grad_w_down = t_times(inner_low, mlp_grad_all)
    grad_inner = times_t(mlp_grad_all, w_down)
    grad_gate_low = (
        grad_inner * up_acts * gate_sigmoid * (1.0 + gate_acts * (1.0 - gate_sigmoid))
    ).astype(jnp.bfloat16)
    grad_up_low = (grad_inner * gate_acts * gate_sigmoid).astype(jnp.bfloat16)
    grad_w_gate = t_times(hidden_all, grad_gate_low)
    grad_w_up = t_times(hidden_all, grad_up_low)
    grad_hidden = grad_output + lax.psum_scatter(
        (times_t(grad_gate_low, w_gate) + times_t(grad_up_low, w_up)).astype(jnp.bfloat16),
        "tensor",
        scatter_dimension=0,
        tiled=True,
    ).astype(jnp.float32)
    grad_attn, grad_gain_attn_part = post_norm_back(grad_hidden, a_unit, a_inv, gain_attn)
    attn_grad_all = lax.all_gather(grad_attn.astype(jnp.bfloat16), "tensor", axis=0, tiled=True)
    grad_w_out = t_times(mixed_low, attn_grad_all)
    grad_mixed = times_t(attn_grad_all, w_out).astype(jnp.bfloat16)
    grad_q_rot, grad_k_rot, grad_values_low = lax.map(
        attend_back, (queries_low, keys_low, values_heads, segment, log_total, to_heads(grad_mixed))
    )
    grad_q_norm = rotate(grad_q_rot, offsets, -1.0).reshape(row_count, local_width)
    grad_k_norm = rotate(grad_k_rot, offsets, -1.0).reshape(row_count, local_width)
    grad_gain_query_part = jnp.sum(grad_q_norm * q_unit, axis=0)
    grad_gain_key_part = jnp.sum(grad_k_norm * k_unit, axis=0)
    q_scaled = grad_q_norm * gain_query
    k_scaled = grad_k_norm * gain_key
    q_dots, k_dots = lax.psum(
        (jnp.sum(q_scaled * q_unit, axis=1), jnp.sum(k_scaled * k_unit, axis=1)), "tensor"
    )
    grad_queries_low = (q_inv * (q_scaled - q_unit * (q_dots / model_width)[:, None])).astype(
        jnp.bfloat16
    )
    grad_keys_low = (k_inv * (k_scaled - k_unit * (k_dots / model_width)[:, None])).astype(
        jnp.bfloat16
    )
    grad_values_flat = grad_values_low.reshape(row_count, local_width)
    grad_w_query = t_times(gathered, grad_queries_low)
    grad_w_key = t_times(gathered, grad_keys_low)
    grad_w_value = t_times(gathered, grad_values_flat)
    grad_tokens = (
        grad_hidden
        + lax.psum_scatter(
            (
                times_t(grad_queries_low, w_query)
                + times_t(grad_keys_low, w_key)
                + times_t(grad_values_flat, w_value)
            ).astype(jnp.bfloat16),
            "tensor",
            scatter_dimension=0,
            tiled=True,
        ).astype(jnp.float32)
    ).astype(jnp.bfloat16)
    tensor_start = lax.axis_index("tensor") * local_width
    zero_row = jnp.zeros((model_width,), jnp.float32)
    q_full = lax.dynamic_update_slice(zero_row, grad_gain_query_part, (tensor_start,))
    k_full = lax.dynamic_update_slice(zero_row, grad_gain_key_part, (tensor_start,))
    gain_stack = jnp.stack([q_full, k_full, grad_gain_attn_part, grad_gain_mlp_part])
    gain_total = lax.psum(gain_stack, ("dp", "tensor"))
    grad_gain_query = lax.dynamic_slice(gain_total[0], (tensor_start,), (local_width,))
    grad_gain_key = lax.dynamic_slice(gain_total[1], (tensor_start,), (local_width,))
    summed = (
        lax.psum_scatter(
            grad_w_query.astype(jnp.bfloat16), "dp", scatter_dimension=0, tiled=True
        ).astype(jnp.float32),
        lax.psum_scatter(
            grad_w_key.astype(jnp.bfloat16), "dp", scatter_dimension=0, tiled=True
        ).astype(jnp.float32),
        lax.psum_scatter(
            grad_w_value.astype(jnp.bfloat16), "dp", scatter_dimension=0, tiled=True
        ).astype(jnp.float32),
        lax.psum_scatter(
            grad_w_out.astype(jnp.bfloat16), "dp", scatter_dimension=1, tiled=True
        ).astype(jnp.float32),
        lax.psum_scatter(
            grad_w_gate.astype(jnp.bfloat16), "dp", scatter_dimension=0, tiled=True
        ).astype(jnp.float32),
        lax.psum_scatter(
            grad_w_up.astype(jnp.bfloat16), "dp", scatter_dimension=0, tiled=True
        ).astype(jnp.float32),
        lax.psum_scatter(
            grad_w_down.astype(jnp.bfloat16), "dp", scatter_dimension=1, tiled=True
        ).astype(jnp.float32),
    )
    return (
        output,
        grad_tokens,
        summed[0],
        summed[1],
        summed[2],
        summed[3],
        summed[4],
        summed[5],
        summed[6],
        grad_gain_query,
        grad_gain_key,
        gain_total[2],
        gain_total[3],
    )


def solution(mesh):
    placed = (
        P(("dp", "tensor"), None),
        P("dp", None),
        P(None, "tensor"),
        P(None, "tensor"),
        P(None, "tensor"),
        P("tensor", None),
        P(None, "tensor"),
        P(None, "tensor"),
        P("tensor", None),
        P("tensor"),
        P("tensor"),
        P(),
        P(),
        P(("dp", "tensor"), None),
    )
    return jax.shard_map(
        body,
        mesh=mesh,
        in_specs=placed,
        out_specs=(
            P(("dp", "tensor"), None),
            P(("dp", "tensor"), None),
            P("dp", "tensor"),
            P("dp", "tensor"),
            P("dp", "tensor"),
            P("tensor", "dp"),
            P("dp", "tensor"),
            P("dp", "tensor"),
            P("tensor", "dp"),
            P("tensor"),
            P("tensor"),
            P(),
            P(),
        ),
        check_vma=False,
    )
```

profile of v0, /device:TPU:0, one launch (start us, length us, event | category | flops | bytes accessed | tf_op | source)
XLA Modules:
  0.0 1118.6 jit_solution(15427189430564919261)
XLA Ops:
  12.3 22.6 %all-gather.5.cloned.1.call-done = bf16[512,2048]{1,0:T(8,128)(2,1)} async-done(((bf16[128,2048]{1,0:T(8,128)(2,1)}), bf16[512,2048]{1,0:T(8,128)(2,1)}) %all-gather.5.cloned.1.call-update) | async-done | bytes 2097168 | tf_op jit(solution)/shard_map/all_gather | solution.py:129
  69.2 32.6 %reduce-scatter.12.cloned.1.call-done = bf16[128,2048]{1,0:T(8,128)(2,1)} async-done(((bf16[512,2048]{1,0:T(8,128)(2,1)}), bf16[128,2048]{1,0:T(8,128)(2,1)}) %reduce-scatter.12.cloned.1.call-update) | async-done | bytes 524304 | tf_op jit(solution)/shard_map/reduce_scatter | solution.py:151
  105.4 22.5 %all-gather.7.cloned.1.call-done = bf16[512,2048]{1,0:T(8,128)(2,1)} async-done(((bf16[128,2048]{1,0:T(8,128)(2,1)}), bf16[512,2048]{1,0:T(8,128)(2,1)}) %all-gather.7.cloned.1.call-update) | async-done | bytes 2097168 | tf_op jit(solution)/shard_map/all_gather | solution.py:160
  127.9 8.5 fusion.52
  136.4 11.7 %multiply_convert_fusion.3 = (bf16[512,2048]{1,0:T(8,128)(2,1)S(1)}, f32[512,2048]{1,0:T(8,128)}) fusion(f32[512,2048]{1,0:T(8,128)S(1)} %fusion.52, bf16[512,2048]{1,0:T(8,128)(2,1)S(1)} %copy-done.40, bf16[2048,2048]{1,0:T(8,128)(2,1)} %param.21), kind=kOutput, calls=%fused_computation.10 | convolution fusion | flops 4301258752 | bytes 20971520 | tf_op jit(solution)/shard_map/dot_general | solution.py:162
  155.3 31.5 %reduce-scatter.14.cloned.1.call-done = bf16[128,2048]{1,0:T(8,128)(2,1)} async-done(((bf16[512,2048]{1,0:T(8,128)(2,1)}), bf16[128,2048]{1,0:T(8,128)(2,1)}) %reduce-scatter.14.cloned.1.call-update) | async-done | bytes 524304 | tf_op jit(solution)/shard_map/reduce_scatter | solution.py:165
  192.2 22.3 %all-gather.9.cloned.1.call-done = bf16[512,2048]{1,0:T(8,128)(2,1)} async-done(((bf16[128,2048]{1,0:T(8,128)(2,1)}), bf16[512,2048]{1,0:T(8,128)(2,1)}) %all-gather.9.cloned.1.call-update) | async-done | bytes 2097168 | tf_op jit(solution)/shard_map/all_gather | solution.py:176
  214.5 11.9 %multiply_convert_fusion.1 = (bf16[512,2048]{1,0:T(8,128)(2,1)S(1)}, bf16[512,2048]{1,0:T(8,128)(2,1)S(1)}) fusion(f32[512,2048]{1,0:T(8,128)} %copy-done.42, f32[512,2048]{1,0:T(8,128)} %get-tuple-element.138, bf16[512,2048]{1,0:T(8,128)(2,1)} %all-gather.9.cloned.1.call-done, bf16[2048,2048]{1,0:T(8,128)(2,1)} %param.22), kind=kOutput, calls=%fused_computation.8 | convolution fusion | flops 4308598784 | bytes 23068672 | tf_op jit(solution)/shard_map/dot_general | solution.py:47
  226.4 8.5 fusion.53
  234.9 9.2 add_convert_fusion.1
  244.2 31.6 %reduce-scatter.16.cloned.1.call-done = bf16[128,2048]{1,0:T(8,128)(2,1)} async-done(((bf16[512,2048]{1,0:T(8,128)(2,1)}), bf16[128,2048]{1,0:T(8,128)(2,1)}) %reduce-scatter.16.cloned.1.call-update) | async-done | bytes 524304 | tf_op jit(solution)/shard_map/reduce_scatter | solution.py:185
  280.5 22.5 %all-gather.11.cloned.1.call-done = bf16[512,2048]{1,0:T(8,128)(2,1)} async-done(((bf16[128,2048]{1,0:T(8,128)(2,1)}), bf16[512,2048]{1,0:T(8,128)(2,1)}) %all-gather.11.cloned.1.call-update) | async-done | bytes 2097168 | tf_op jit(solution)/shard_map/all_gather | solution.py:192
  325.0 5.9 all-reduce
  358.8 10.0 convolution_convert_fusion.2
  369.1 10.1 convolution_convert_fusion.1
  379.3 10.0 convolution_convert_fusion
  389.5 40.7 %psum.39 = f32[4,2048]{1,0:T(4,128)S(1)} all-reduce(f32[4,2048]{1,0:T(4,128)S(1)} %pad_maximum_fusion.8), channel_id=1, replica_groups=mesh['dp'=8,'tensor'=4] {'dp','tensor'}, use_global_device_ids=true, to_apply=%region_33.34 | all-reduce | flops 8192 | bytes 65536 | tf_op jit(solution)/shard_map/psum | solution.py:235
  433.8 43.0 %reduce-scatter.22.cloned.1.call-done = bf16[256,512]{0,1:T(8,128)(2,1)} async-done(((bf16[2048,512]{0,1:T(8,128)(2,1)}), bf16[256,512]{0,1:T(8,128)(2,1)}) %reduce-scatter.22.cloned.1.call-update) | async-done | bytes 262160 | tf_op jit(solution)/shard_map/reduce_scatter | solution.py:242
  478.8 69.0 %reduce-scatter.24.cloned.1.call-done = bf16[256,512]{0,1:T(8,128)(2,1)} async-done(((bf16[2048,512]{0,1:T(8,128)(2,1)}), bf16[256,512]{0,1:T(8,128)(2,1)}) %reduce-scatter.24.cloned.1.call-update) | async-done | bytes 262160 | tf_op jit(solution)/shard_map/reduce_scatter | solution.py:245
  549.6 69.2 %reduce-scatter.26.cloned.1.call-done = bf16[512,256]{1,0:T(8,128)(2,1)} async-done(((bf16[512,2048]{1,0:T(8,128)(2,1)}), bf16[512,256]{1,0:T(8,128)(2,1)}) %reduce-scatter.26.cloned.1.call-update) | async-done | bytes 262160 | tf_op jit(solution)/shard_map/reduce_scatter | solution.py:248
  620.6 31.8 %reduce-scatter.18.cloned.1.call-done = bf16[128,2048]{1,0:T(8,128)(2,1)} async-done(((bf16[512,2048]{1,0:T(8,128)(2,1)}), bf16[128,2048]{1,0:T(8,128)(2,1)}) %reduce-scatter.18.cloned.1.call-update) | async-done | bytes 524304 | tf_op jit(solution)/shard_map/reduce_scatter | solution.py:219
  654.4 150.6 %reduce-scatter.28.cloned.1.call-done = bf16[256,2048]{1,0:T(8,128)(2,1)} async-done(((bf16[2048,2048]{1,0:T(8,128)(2,1)}), bf16[256,2048]{1,0:T(8,128)(2,1)}) %reduce-scatter.28.cloned.1.call-update) | async-done | bytes 1048592 | tf_op jit(solution)/shard_map/reduce_scatter | solution.py:251
  807.8 149.2 %reduce-scatter.30.cloned.1.call-done = bf16[256,2048]{1,0:T(8,128)(2,1)} async-done(((bf16[2048,2048]{1,0:T(8,128)(2,1)}), bf16[256,2048]{1,0:T(8,128)(2,1)}) %reduce-scatter.30.cloned.1.call-update) | async-done | bytes 1048592 | tf_op jit(solution)/shard_map/reduce_scatter | solution.py:254
  959.8 149.1 %reduce-scatter.32.cloned.1.call-done = bf16[2048,256]{1,0:T(8,128)(2,1)} async-done(((bf16[2048,2048]{1,0:T(8,128)(2,1)}), bf16[2048,256]{1,0:T(8,128)(2,1)}) %reduce-scatter.32.cloned.1.call-update) | async-done | bytes 1048592 | tf_op jit(solution)/shard_map/reduce_scatter | solution.py:257
  (205 shorter events, 129.7 us)
Async XLA Ops:
  7.2 27.7 %copy-start = (bf16[2048,512]{1,0:T(8,128)(2,1)S(1)}, bf16[2048,512]{1,0:T(8,128)(2,1)}, u32[]{:S(2)}) copy-start(bf16[2048,512]{1,0:T(8,128)(2,1)} %param.16) | copy-start | bytes 6291460
  7.2 27.7 %all-gather.5.cloned.1.call-start = ((), (), s32[]{:S(2)}) async-start(), calls=%async_computation.11 | async-start | bytes 2621440 | tf_op jit(solution)/shard_map/all_gather | solution.py:129
  7.9 93.8 %reduce-scatter.12.cloned.1.call-start = ((), (), s32[]{:S(2)}) async-start(), calls=%async_computation.12 | async-start | bytes 2621440 | tf_op jit(solution)/shard_map/reduce_scatter | solution.py:151
  69.1 33.9 %copy-start.5 = (bf16[128,2048]{1,0:T(8,128)(2,1)S(1)}, bf16[128,2048]{1,0:T(8,128)(2,1)}, u32[]{:S(2)}) copy-start(bf16[128,2048]{1,0:T(8,128)(2,1)} %param.14) | copy-start | bytes 1572868
  69.1 33.9 %copy-start.30 = (f32[2048]{0:T(1024)S(1)}, f32[2048]{0:T(1024)}, u32[]{:S(2)}) copy-start(f32[2048]{0:T(1024)} %param.25) | copy-start | bytes 24580
  69.1 58.8 %all-gather.7.cloned.1.call-start = ((), (), s32[]{:S(2)}) async-start(), calls=%async_computation.13 | async-start | bytes 2621440 | tf_op jit(solution)/shard_map/all_gather | solution.py:160
  105.1 81.7 %reduce-scatter.14.cloned.1.call-start = ((), (), s32[]{:S(2)}) async-start(), calls=%async_computation.14 | async-start | bytes 2621440 | tf_op jit(solution)/shard_map/reduce_scatter | solution.py:165
  127.9 21.6 %slice-start = ((s8[8388608]{0:T(1024)(128)(4,1)}), s8[4194304]{0:T(1024)(128)(4,1)S(1)}, s32[]{:S(2)}) async-start(s8[8388608]{0:T(1024)(128)(4,1)} %bitcast.128), calls=%async_computation.26 | async-start | bytes 8388608
  155.2 32.9 %copy-start.3 = (bf16[128,2048]{1,0:T(8,128)(2,1)S(1)}, bf16[128,2048]{1,0:T(8,128)(2,1)}, u32[]{:S(2)}) copy-start(bf16[128,2048]{1,0:T(8,128)(2,1)} %param.27) | copy-start | bytes 1572868
  155.2 32.9 %copy-start.31 = (f32[2048]{0:T(1024)S(1)}, f32[2048]{0:T(1024)}, u32[]{:S(2)}) copy-start(f32[2048]{0:T(1024)} %param.26) | copy-start | bytes 24580
  155.2 59.3 %all-gather.9.cloned.1.call-start = ((), (), s32[]{:S(2)}) async-start(), calls=%async_computation.15 | async-start | bytes 2621440 | tf_op jit(solution)/shard_map/all_gather | solution.py:176
  191.8 84.0 %reduce-scatter.16.cloned.1.call-start = ((), (), s32[]{:S(2)}) async-start(), calls=%async_computation.16 | async-start | bytes 2621440 | tf_op jit(solution)/shard_map/reduce_scatter | solution.py:185
  244.1 31.6 %copy-start.4 = (bf16[128,2048]{1,0:T(8,128)(2,1)S(1)}, bf16[128,2048]{1,0:T(8,128)(2,1)}, u32[]{:S(2)}) copy-start(bf16[128,2048]{1,0:T(8,128)(2,1)} %reduce-scatter.12.cloned.1.call-done) | copy-start | bytes 1572868
  244.1 58.8 %all-gather.11.cloned.1.call-start = ((), (), s32[]{:S(2)}) async-start(), calls=%async_computation.17 | async-start | bytes 2621440 | tf_op jit(solution)/shard_map/all_gather | solution.py:192
  280.2 151.7 %reduce-scatter.20.cloned.1.call-start = ((), (), s32[]{:S(2)}) async-start(), calls=%async_computation.19 | async-start | bytes 2359296 | tf_op jit(solution)/shard_map/reduce_scatter | solution.py:239
  280.5 26.2 %copy-start.29 = (bf16[512,512]{0,1:T(8,128)(2,1)S(1)}, bf16[512,512]{0,1:T(8,128)(2,1)}, u32[]{:S(2)}) copy-start(bf16[512,512]{0,1:T(8,128)(2,1)} %copy-done.28) | copy-start | bytes 1572868
  335.7 141.2 %reduce-scatter.22.cloned.1.call-start = ((), (), s32[]{:S(2)}) async-start(), calls=%async_computation.20 | async-start | bytes 2359296 | tf_op jit(solution)/shard_map/reduce_scatter | solution.py:242
  341.1 206.7 %reduce-scatter.24.cloned.1.call-start = ((), (), s32[]{:S(2)}) async-start(), calls=%async_computation.21 | async-start | bytes 2359296 | tf_op jit(solution)/shard_map/reduce_scatter | solution.py:245
  347.9 270.9 %reduce-scatter.26.cloned.1.call-start = ((), (), s32[]{:S(2)}) async-start(), calls=%async_computation.22 | async-start | bytes 2359296 | tf_op jit(solution)/shard_map/reduce_scatter | solution.py:248
  352.5 299.8 %reduce-scatter.18.cloned.1.call-start = ((), (), s32[]{:S(2)}) async-start(), calls=%async_computation.18 | async-start | bytes 2621440 | tf_op jit(solution)/shard_map/reduce_scatter | solution.py:219
  358.7 446.3 %reduce-scatter.28.cloned.1.call-start = ((), (), s32[]{:S(2)}) async-start(), calls=%async_computation.23 | async-start | bytes 9437184 | tf_op jit(solution)/shard_map/reduce_scatter | solution.py:251
  368.8 588.2 %reduce-scatter.30.cloned.1.call-start = ((), (), s32[]{:S(2)}) async-start(), calls=%async_computation.24 | async-start | bytes 9437184 | tf_op jit(solution)/shard_map/reduce_scatter | solution.py:254
  379.2 729.7 %reduce-scatter.32.cloned.1.call-start = ((), (), s32[]{:S(2)}) async-start(), calls=%async_computation.25 | async-start | bytes 9437184 | tf_op jit(solution)/shard_map/reduce_scatter | solution.py:257
  389.3 263.0 %copy-start.6 = (bf16[128,2048]{1,0:T(8,128)(2,1)S(1)}, bf16[128,2048]{1,0:T(8,128)(2,1)}, u32[]{:S(2)}) copy-start(bf16[128,2048]{1,0:T(8,128)(2,1)} %reduce-scatter.16.cloned.1.call-done) | copy-start | bytes 1572868
  (39 other events, 126.2 us)
Sparse Core Ops, SparseCore 0:
  9.6 25.2 all-gather.4
  69.2 32.4 reduce-scatter.11
  105.3 22.5 all-gather.6
  155.3 31.4 reduce-scatter.13
  191.9 22.5 all-gather.8
  244.3 31.4 reduce-scatter.15
  280.4 22.5 all-gather.10
  335.8 69.3 reduce-scatter.19
  409.7 67.1 reduce-scatter.21
  480.7 67.0 reduce-scatter.23
  551.7 67.0 reduce-scatter.25
  621.9 30.3 reduce-scatter.17
  656.0 149.0 reduce-scatter.27
  808.9 148.0 reduce-scatter.29
  960.5 148.3 reduce-scatter.31
where the time goes:
time: 1130 us; the launch traced here: 1120 us
  waiting for transfers between devices  848 us (75%)
  matrix products  125 us (11%)
  blocking collectives  52.4 us (5%)
  other arithmetic  48.9 us (4%)
  local copies, waits for them, and re-layouts  26.8 us (2%)
  between operations  15 us (1%)
    reduce_scatter x1, waiting for transfers between devices, body(): lax.psum_scatter(grad_w_gate.astype(jnp.bfloat16), 'dp', scatter_dimensio...  151 us
    reduce_scatter x1, waiting for transfers between devices, body(): lax.psum_scatter(grad_w_up.astype(jnp.bfloat16), 'dp', scatter_dimension=...  149 us
    reduce_scatter x1, waiting for transfers between devices, body(): lax.psum_scatter(grad_w_down.astype(jnp.bfloat16), 'dp', scatter_dimensio...  149 us
    reduce_scatter x1, waiting for transfers between devices, body(): lax.psum_scatter(grad_w_out.astype(jnp.bfloat16), 'dp', scatter_dimension...  69.2 us
    reduce_scatter x1, waiting for transfers between devices, body(): lax.psum_scatter(grad_w_value.astype(jnp.bfloat16), 'dp', scatter_dimensi...  69 us
    reduce_scatter x1, waiting for transfers between devices, body(): lax.psum_scatter(grad_w_key.astype(jnp.bfloat16), 'dp', scatter_dimension...  43 us
    dot_general x7, matrix products, t_times(): lax.dot_general(left_mat, right_mat, (((0,), (0,)), ((), ())), preferred_...  42.3 us
    psum x1, blocking collectives, body(): gain_total = lax.psum(gain_stack, ('dp', 'tensor'))  40.7 us
  transfers between devices with their start and end apart: 15, of which 14 were waited for; matrix products, arithmetic and copies ran while one was open for 6% of the time, Pallas kernels for 0%

commit v1 on v0

--- a/solution.py
+++ b/solution.py
@@ -232,7 +232,13 @@
     q_full = lax.dynamic_update_slice(zero_row, grad_gain_query_part, (tensor_start,))
     k_full = lax.dynamic_update_slice(zero_row, grad_gain_key_part, (tensor_start,))
     gain_stack = jnp.stack([q_full, k_full, grad_gain_attn_part, grad_gain_mlp_part])
-    gain_total = lax.psum(gain_stack, ("dp", "tensor"))
+
+    def slot_wait(m, dev_axis):
+        r2 = lax.all_gather(m, dev_axis)
+        b_now = jnp.sum(r2, axis=0)
+        return b_now
+
+    gain_total = slot_wait(gain_stack, ("dp", "tensor"))
     grad_gain_query = lax.dynamic_slice(gain_total[0], (tensor_start,), (local_width,))
     grad_gain_key = lax.dynamic_slice(gain_total[1], (tensor_start,), (local_width,))
     summed = (

time: 1130 us -> 1170 us (1.035)
  waiting for transfers between devices: 848 us -> 934 us
  blocking collectives: 52.4 us -> 11.7 us
    reduce_scatter x1, waiting for transfers between devices: 0.01 us -> 58.1 us  [body(): lax.psum_scatter(grad_w_query.astype(jnp.bfloat16), 'dp', scatter_dimensi...]
    psum x1 -> x0, blocking collectives: 40.7 us -> none  [body(): gain_total = lax.psum(gain_stack, ('dp', 'tensor'))]
    reduce_scatter x1, waiting for transfers between devices: 43 us -> 69.8 us  [body(): lax.psum_scatter(grad_w_key.astype(jnp.bfloat16), 'dp', scatter_dimension...]
  transfers between devices with their start and end apart: 15 -> 16, of which waited for: 14 -> 15; matrix products, arithmetic and copies ran while one was open for 6% -> 7% of each run, Pallas kernels for 0% -> 0%
where the time goes in v1:
time: 1170 us
  waiting for transfers between devices  934 us (80%)
  matrix products  125 us (11%)
  other arithmetic  51 us (4%)
  local copies, waits for them, and re-layouts  26.8 us (2%)
  between operations  15.1 us (1%)
    reduce_scatter x1, waiting for transfers between devices, body(): lax.psum_scatter(grad_w_gate.astype(jnp.bfloat16), 'dp', scatter_dimensio...  150 us
    reduce_scatter x1, waiting for transfers between devices, body(): lax.psum_scatter(grad_w_down.astype(jnp.bfloat16), 'dp', scatter_dimensio...  149 us
    reduce_scatter x1, waiting for transfers between devices, body(): lax.psum_scatter(grad_w_up.astype(jnp.bfloat16), 'dp', scatter_dimension=...  149 us
    reduce_scatter x1, waiting for transfers between devices, body(): lax.psum_scatter(grad_w_key.astype(jnp.bfloat16), 'dp', scatter_dimension...  69.8 us
    reduce_scatter x1, waiting for transfers between devices, body(): lax.psum_scatter(grad_w_value.astype(jnp.bfloat16), 'dp', scatter_dimensi...  69.4 us
    reduce_scatter x1, waiting for transfers between devices, body(): lax.psum_scatter(grad_w_out.astype(jnp.bfloat16), 'dp', scatter_dimension...  69.1 us
    reduce_scatter x1, waiting for transfers between devices, body(): lax.psum_scatter(grad_w_query.astype(jnp.bfloat16), 'dp', scatter_dimensi...  58.1 us
    dot_general x7, matrix products, t_times(): lax.dot_general(left_mat, right_mat, (((0,), (0,)), ((), ())), preferred_...  42.2 us
  transfers between devices with their start and end apart: 16, of which 15 were waited for; matrix products, arithmetic and copies ran while one was open for 7% of the time, Pallas kernels for 0%

profile of v1, /device:TPU:0, one launch (start us, length us, event | category | flops | bytes accessed | tf_op | source)
XLA Modules:
  0.0 1165.3 jit_solution(8825576092158362530)
XLA Ops:
  12.3 22.6 %all-gather.8.cloned.1.call-done = bf16[512,2048]{1,0:T(8,128)(2,1)} async-done(((bf16[128,2048]{1,0:T(8,128)(2,1)}), bf16[512,2048]{1,0:T(8,128)(2,1)}) %all-gather.8.cloned.1.call-update) | async-done | bytes 2097168 | tf_op jit(solution)/shard_map/all_gather | solution.py:129
  69.2 32.6 %reduce-scatter.12.cloned.1.call-done = bf16[128,2048]{1,0:T(8,128)(2,1)} async-done(((bf16[512,2048]{1,0:T(8,128)(2,1)}), bf16[128,2048]{1,0:T(8,128)(2,1)}) %reduce-scatter.12.cloned.1.call-update) | async-done | bytes 524304 | tf_op jit(solution)/shard_map/reduce_scatter | solution.py:151
  105.4 22.5 %all-gather.10.cloned.1.call-done = bf16[512,2048]{1,0:T(8,128)(2,1)} async-done(((bf16[128,2048]{1,0:T(8,128)(2,1)}), bf16[512,2048]{1,0:T(8,128)(2,1)}) %all-gather.10.cloned.1.call-update) | async-done | bytes 2097168 | tf_op jit(solution)/shard_map/all_gather | solution.py:160
  127.9 8.5 fusion.52
  136.4 11.7 %multiply_convert_fusion.3 = (bf16[512,2048]{1,0:T(8,128)(2,1)S(1)}, f32[512,2048]{1,0:T(8,128)}) fusion(f32[512,2048]{1,0:T(8,128)S(1)} %fusion.52, bf16[512,2048]{1,0:T(8,128)(2,1)S(1)} %copy-done.40, bf16[2048,2048]{1,0:T(8,128)(2,1)} %param.21), kind=kOutput, calls=%fused_computation.10 | convolution fusion | flops 4301258752 | bytes 20971520 | tf_op jit(solution)/shard_map/dot_general | solution.py:162
  155.3 31.5 %reduce-scatter.14.cloned.1.call-done = bf16[128,2048]{1,0:T(8,128)(2,1)} async-done(((bf16[512,2048]{1,0:T(8,128)(2,1)}), bf16[128,2048]{1,0:T(8,128)(2,1)}) %reduce-scatter.14.cloned.1.call-update) | async-done | bytes 524304 | tf_op jit(solution)/shard_map/reduce_scatter | solution.py:165
  192.2 22.3 %all-gather.12.cloned.1.call-done = bf16[512,2048]{1,0:T(8,128)(2,1)} async-done(((bf16[128,2048]{1,0:T(8,128)(2,1)}), bf16[512,2048]{1,0:T(8,128)(2,1)}) %all-gather.12.cloned.1.call-update) | async-done | bytes 2097168 | tf_op jit(solution)/shard_map/all_gather | solution.py:176
  214.5 11.9 %multiply_convert_fusion.1 = (bf16[512,2048]{1,0:T(8,128)(2,1)S(1)}, bf16[512,2048]{1,0:T(8,128)(2,1)S(1)}) fusion(f32[512,2048]{1,0:T(8,128)} %copy-done.42, f32[512,2048]{1,0:T(8,128)} %get-tuple-element.151, bf16[512,2048]{1,0:T(8,128)(2,1)} %all-gather.12.cloned.1.call-done, bf16[2048,2048]{1,0:T(8,128)(2,1)} %param.22), kind=kOutput, calls=%fused_computation.8 | convolution fusion | flops 4308598784 | bytes 23068672 | tf_op jit(solution)/shard_map/dot_general | solution.py:47
  226.5 8.5 fusion.53
  234.9 9.2 add_convert_fusion.1
  244.2 31.6 %reduce-scatter.16.cloned.1.call-done = bf16[128,2048]{1,0:T(8,128)(2,1)} async-done(((bf16[512,2048]{1,0:T(8,128)(2,1)}), bf16[128,2048]{1,0:T(8,128)(2,1)}) %reduce-scatter.16.cloned.1.call-update) | async-done | bytes 524304 | tf_op jit(solution)/shard_map/reduce_scatter | solution.py:185
  280.5 22.5 %all-gather.14.cloned.1.call-done = bf16[512,2048]{1,0:T(8,128)(2,1)} async-done(((bf16[128,2048]{1,0:T(8,128)(2,1)}), bf16[512,2048]{1,0:T(8,128)(2,1)}) %all-gather.14.cloned.1.call-update) | async-done | bytes 2097168 | tf_op jit(solution)/shard_map/all_gather | solution.py:192
  325.8 5.9 all-reduce
  359.6 10.0 convolution_convert_fusion.2
  370.0 10.0 convolution_convert_fusion.1
  380.1 10.0 convolution_convert_fusion
  393.4 58.1 %reduce-scatter.20.cloned.1.call-done = bf16[256,512]{0,1:T(8,128)(2,1)} async-done(((bf16[2048,512]{0,1:T(8,128)(2,1)}), bf16[256,512]{0,1:T(8,128)(2,1)}) %reduce-scatter.20.cloned.1.call-update) | async-done | bytes 262160 | tf_op jit(solution)/shard_map/reduce_scatter | solution.py:245
  453.5 69.8 %reduce-scatter.22.cloned.1.call-done = bf16[256,512]{0,1:T(8,128)(2,1)} async-done(((bf16[2048,512]{0,1:T(8,128)(2,1)}), bf16[256,512]{0,1:T(8,128)(2,1)}) %reduce-scatter.22.cloned.1.call-update) | async-done | bytes 262160 | tf_op jit(solution)/shard_map/reduce_scatter | solution.py:248
  525.2 69.4 %reduce-scatter.24.cloned.1.call-done = bf16[256,512]{0,1:T(8,128)(2,1)} async-done(((bf16[2048,512]{0,1:T(8,128)(2,1)}), bf16[256,512]{0,1:T(8,128)(2,1)}) %reduce-scatter.24.cloned.1.call-update) | async-done | bytes 262160 | tf_op jit(solution)/shard_map/reduce_scatter | solution.py:251
  596.5 69.1 %reduce-scatter.26.cloned.1.call-done = bf16[512,256]{1,0:T(8,128)(2,1)} async-done(((bf16[512,2048]{1,0:T(8,128)(2,1)}), bf16[512,256]{1,0:T(8,128)(2,1)}) %reduce-scatter.26.cloned.1.call-update) | async-done | bytes 262160 | tf_op jit(solution)/shard_map/reduce_scatter | solution.py:254
  667.4 31.9 %reduce-scatter.18.cloned.1.call-done = bf16[128,2048]{1,0:T(8,128)(2,1)} async-done(((bf16[512,2048]{1,0:T(8,128)(2,1)}), bf16[128,2048]{1,0:T(8,128)(2,1)}) %reduce-scatter.18.cloned.1.call-update) | async-done | bytes 524304 | tf_op jit(solution)/shard_map/reduce_scatter | solution.py:219
  701.3 150.5 %reduce-scatter.28.cloned.1.call-done = bf16[256,2048]{1,0:T(8,128)(2,1)} async-done(((bf16[2048,2048]{1,0:T(8,128)(2,1)}), bf16[256,2048]{1,0:T(8,128)(2,1)}) %reduce-scatter.28.cloned.1.call-update) | async-done | bytes 1048592 | tf_op jit(solution)/shard_map/reduce_scatter | solution.py:257
  854.6 149.1 %reduce-scatter.30.cloned.1.call-done = bf16[256,2048]{1,0:T(8,128)(2,1)} async-done(((bf16[2048,2048]{1,0:T(8,128)(2,1)}), bf16[256,2048]{1,0:T(8,128)(2,1)}) %reduce-scatter.30.cloned.1.call-update) | async-done | bytes 1048592 | tf_op jit(solution)/shard_map/reduce_scatter | solution.py:260
  1006.5 149.1 %reduce-scatter.32.cloned.1.call-done = bf16[2048,256]{1,0:T(8,128)(2,1)} async-done(((bf16[2048,2048]{1,0:T(8,128)(2,1)}), bf16[2048,256]{1,0:T(8,128)(2,1)}) %reduce-scatter.32.cloned.1.call-update) | async-done | bytes 1048592 | tf_op jit(solution)/shard_map/reduce_scatter | solution.py:263
  (208 shorter events, 131.8 us)
Async XLA Ops:
  7.2 27.7 %copy-start = (bf16[2048,512]{1,0:T(8,128)(2,1)S(1)}, bf16[2048,512]{1,0:T(8,128)(2,1)}, u32[]{:S(2)}) copy-start(bf16[2048,512]{1,0:T(8,128)(2,1)} %param.16) | copy-start | bytes 6291460
  7.2 27.7 %all-gather.8.cloned.1.call-start = ((), (), s32[]{:S(2)}) async-start(), calls=%async_computation.11 | async-start | bytes 2621440 | tf_op jit(solution)/shard_map/all_gather | solution.py:129
  7.9 93.8 %reduce-scatter.12.cloned.1.call-start = ((), (), s32[]{:S(2)}) async-start(), calls=%async_computation.12 | async-start | bytes 2621440 | tf_op jit(solution)/shard_map/reduce_scatter | solution.py:151
  69.1 33.9 %copy-start.5 = (bf16[128,2048]{1,0:T(8,128)(2,1)S(1)}, bf16[128,2048]{1,0:T(8,128)(2,1)}, u32[]{:S(2)}) copy-start(bf16[128,2048]{1,0:T(8,128)(2,1)} %param.14) | copy-start | bytes 1572868
  69.1 33.9 %copy-start.30 = (f32[2048]{0:T(1024)S(1)}, f32[2048]{0:T(1024)}, u32[]{:S(2)}) copy-start(f32[2048]{0:T(1024)} %param.25) | copy-start | bytes 24580
  69.1 58.8 %all-gather.10.cloned.1.call-start = ((), (), s32[]{:S(2)}) async-start(), calls=%async_computation.13 | async-start | bytes 2621440 | tf_op jit(solution)/shard_map/all_gather | solution.py:160
  105.1 81.7 %reduce-scatter.14.cloned.1.call-start = ((), (), s32[]{:S(2)}) async-start(), calls=%async_computation.14 | async-start | bytes 2621440 | tf_op jit(solution)/shard_map/reduce_scatter | solution.py:165
  155.2 32.9 %copy-start.3 = (bf16[128,2048]{1,0:T(8,128)(2,1)S(1)}, bf16[128,2048]{1,0:T(8,128)(2,1)}, u32[]{:S(2)}) copy-start(bf16[128,2048]{1,0:T(8,128)(2,1)} %param.27) | copy-start | bytes 1572868
  155.2 32.9 %copy-start.31 = (f32[2048]{0:T(1024)S(1)}, f32[2048]{0:T(1024)}, u32[]{:S(2)}) copy-start(f32[2048]{0:T(1024)} %param.26) | copy-start | bytes 24580
  155.2 59.3 %all-gather.12.cloned.1.call-start = ((), (), s32[]{:S(2)}) async-start(), calls=%async_computation.15 | async-start | bytes 2621440 | tf_op jit(solution)/shard_map/all_gather | solution.py:176
  191.8 84.0 %reduce-scatter.16.cloned.1.call-start = ((), (), s32[]{:S(2)}) async-start(), calls=%async_computation.16 | async-start | bytes 2621440 | tf_op jit(solution)/shard_map/reduce_scatter | solution.py:185
  244.1 31.6 %copy-start.4 = (bf16[128,2048]{1,0:T(8,128)(2,1)S(1)}, bf16[128,2048]{1,0:T(8,128)(2,1)}, u32[]{:S(2)}) copy-start(bf16[128,2048]{1,0:T(8,128)(2,1)} %reduce-scatter.12.cloned.1.call-done) | copy-start | bytes 1572868
  244.1 58.8 %all-gather.14.cloned.1.call-start = ((), (), s32[]{:S(2)}) async-start(), calls=%async_computation.17 | async-start | bytes 2621440 | tf_op jit(solution)/shard_map/all_gather | solution.py:192
  280.2 109.9 %all-gather.16.cloned.1.call-start = ((), (), s32[]{:S(2)}) async-start(), calls=%async_computation.26 | async-start | bytes 1081344 | tf_op jit(solution)/shard_map/all_gather | solution.py:237
  280.5 26.2 %copy-start.29 = (bf16[512,512]{0,1:T(8,128)(2,1)S(1)}, bf16[512,512]{0,1:T(8,128)(2,1)}, u32[]{:S(2)}) copy-start(bf16[512,512]{0,1:T(8,128)(2,1)} %copy-done.28) | copy-start | bytes 1572868
  325.8 125.8 %reduce-scatter.20.cloned.1.call-start = ((), (), s32[]{:S(2)}) async-start(), calls=%async_computation.19 | async-start | bytes 2359296 | tf_op jit(solution)/shard_map/reduce_scatter | solution.py:245
  336.6 186.7 %reduce-scatter.22.cloned.1.call-start = ((), (), s32[]{:S(2)}) async-start(), calls=%async_computation.20 | async-start | bytes 2359296 | tf_op jit(solution)/shard_map/reduce_scatter | solution.py:248
  341.9 252.7 %reduce-scatter.24.cloned.1.call-start = ((), (), s32[]{:S(2)}) async-start(), calls=%async_computation.21 | async-start | bytes 2359296 | tf_op jit(solution)/shard_map/reduce_scatter | solution.py:251
  348.8 316.8 %reduce-scatter.26.cloned.1.call-start = ((), (), s32[]{:S(2)}) async-start(), calls=%async_computation.22 | async-start | bytes 2359296 | tf_op jit(solution)/shard_map/reduce_scatter | solution.py:254
  353.4 345.8 %reduce-scatter.18.cloned.1.call-start = ((), (), s32[]{:S(2)}) async-start(), calls=%async_computation.18 | async-start | bytes 2621440 | tf_op jit(solution)/shard_map/reduce_scatter | solution.py:219
  359.6 492.3 %reduce-scatter.28.cloned.1.call-start = ((), (), s32[]{:S(2)}) async-start(), calls=%async_computation.23 | async-start | bytes 9437184 | tf_op jit(solution)/shard_map/reduce_scatter | solution.py:257
  369.7 634.1 %reduce-scatter.30.cloned.1.call-start = ((), (), s32[]{:S(2)}) async-start(), calls=%async_computation.24 | async-start | bytes 9437184 | tf_op jit(solution)/shard_map/reduce_scatter | solution.py:260
  380.0 775.6 %reduce-scatter.32.cloned.1.call-start = ((), (), s32[]{:S(2)}) async-start(), calls=%async_computation.25 | async-start | bytes 9437184 | tf_op jit(solution)/shard_map/reduce_scatter | solution.py:263
  390.1 309.1 %copy-start.6 = (bf16[128,2048]{1,0:T(8,128)(2,1)S(1)}, bf16[128,2048]{1,0:T(8,128)(2,1)}, u32[]{:S(2)}) copy-start(bf16[128,2048]{1,0:T(8,128)(2,1)} %reduce-scatter.16.cloned.1.call-done) | copy-start | bytes 1572868
  (40 other events, 147.9 us)
Sparse Core Ops, SparseCore 0:
  9.6 25.2 all-gather.7
  69.2 32.5 reduce-scatter.11
  105.3 22.5 all-gather.9
  155.3 31.4 reduce-scatter.13
  191.9 22.5 all-gather.11
  244.3 31.4 reduce-scatter.15
  280.4 22.5 all-gather.13
  325.9 53.6 all-gather.15
  384.1 67.3 reduce-scatter.19
  455.9 67.2 reduce-scatter.21
  527.2 67.3 reduce-scatter.23
  598.4 67.1 reduce-scatter.25
  668.8 30.3 reduce-scatter.17
  702.7 149.0 reduce-scatter.27
  855.7 147.9 reduce-scatter.29
  1007.2 148.3 reduce-scatter.31
